TPU v7x, 32 devices: a whole 2x2x4 slice. The times are simulated.
32 devices in a mesh: seq: 8 (over y, x, core), exp: 4 (over z).
Axes of the slice: x: 2, y: 2, z: 4, core: 2. Of those that a mesh axis runs over, the one named last changes fastest.
Arguments:
- layer_input: bfloat16 [4, 4096, 768], P('exp', 'seq'), may hold values from -6 to 6
- token_ids: int32 [4, 4096], P('exp', 'seq'), may hold values from 0 to 8007, as said below
- segment_ids: int32 [4, 4096], P('exp'), may hold values from 0 to 7, never falling along the last dimension, each value on 1 to 1024 neighbouring positions
- hash_table: int32 [8008], replicated, may hold values from 0 to 3, as said below
- first_gain: float32 [768], replicated, may hold values from 0.25 to 1.75
- first_bias: float32 [768], replicated, may hold values from -1.5 to 1.5
- second_gain: float32 [768], replicated, may hold values from 0.25 to 1.75
- second_bias: float32 [768], replicated, may hold values from -1.5 to 1.5
- w_qkv: bfloat16 [768, 2304], replicated, may hold values from -0.21875 to 0.21875
- w_out: bfloat16 [768, 768], replicated, may hold values from -3 to 3
- w_up: bfloat16 [4, 768, 3072], P('exp'), may hold values from -0.21875 to 0.21875
- w_down: bfloat16 [4, 3072, 768], P('exp'), may hold values from -0.109375 to 0.109375
- cotangent: bfloat16 [4, 4096, 768], P('exp', 'seq'), may hold values from -6 to 6
Outputs:
- layer_output: bfloat16 [4, 4096, 768], P('exp', 'seq')
- grad_input: float32 [4, 4096, 768], P('exp', 'seq')
- grad_w_qkv: float32 [768, 2304], replicated
- grad_w_out: float32 [768, 768], replicated
- grad_first_gain: float32 [768], replicated
- grad_first_bias: float32 [768], replicated
- grad_second_gain: float32 [768], replicated
- grad_second_bias: float32 [768], replicated
- grad_w_up: float32 [4, 768, 3072], P('exp')
- grad_w_down: float32 [4, 3072, 768], P('exp')
Inputs may be any that keep to these rules, and one draw needn't show every extreme that they name: `token_ids`: token ids range over the vocabulary. Among the 512 positions that one device holds, hash_table sends exactly 256 to one expert, the same expert on all devices that hold the same positions of their sequences, and the other experts' counts differ from one another by at most one. `hash_table`: every expert is named by 2002 token ids. `segment_ids`: numbers never fall along a sequence; each document holds 1 to 1024 neighbouring positions, and one in every sequence holds exactly 1024.
All inputs are finite; a program needn't handle non-finite values.
Results may differ from a plain program's by a relative error of at most 0.017.
Values may be sent and summed in bfloat16 or wider, within the bound.
No kernel may reach another device: no remote copies, remote signals or barrier semaphores. Data moves between devices by JAX's collectives and lax.ppermute only.
A program may use at most 192 MiB of HBM per device.

v0:
```python
import math
import jax
import jax.numpy as jnp
from jax import lax
from jax.sharding import PartitionSpec as P

HEADS = 12
HEAD_DIM = 64
DOC_MOST = 1024
NEG_BIG = -1e30
EPSILON = 1e-05


def passed_along(block, axis, distance):
    devices = range(lax.axis_size(axis))
    route = [(i - distance, i) for i in devices if i - distance in devices]
    return lax.ppermute(block, axis, route)


def smooth_gate(values):
    return jax.nn.gelu(values, approximate=True)


def norm_rows(values):
    center = values - jnp.mean(values, axis=-1, keepdims=True)
    scale = lax.rsqrt(jnp.mean(center * center, axis=-1, keepdims=True) + EPSILON)
    return (center * scale, scale)


def norm_back(grad_normed, normed, scale):
    inner = jnp.mean(grad_normed * normed, axis=-1, keepdims=True)
    return scale * (grad_normed - jnp.mean(grad_normed, axis=-1, keepdims=True) - normed * inner)


def over_blocks(step, state, pieces, first):
    length = pieces[0].shape[0]
    stride = math.gcd(length, 512)

    def advance(index, current):
        begin = index * stride
        parts = tuple((piece for piece in pieces))
        return step(current, parts, first + begin)

    return lax.fori_loop(0, length // stride, advance, state)


def allowed_pairs(query_pos, query_seg, key_pos, key_seg, limit):
    inside = (key_pos[None, :] >= 0) & (query_pos[:, None] < limit)
    return (
        inside & (key_pos[None, :] <= query_pos[:, None]) & (key_seg[None, :] == query_seg[:, None])
    )


def head_split(rows):
    return rows.reshape(rows.shape[0], HEADS, HEAD_DIM)


def forward_step(queries, query_pos, query_seg, segment_row, limit):
    width = HEADS * HEAD_DIM
    scale = HEAD_DIM ** (-0.5)

    def step(state, parts, first):
        run_max, run_total, weighted = state
        count = parts[0].shape[0]
        key_rows = head_split(parts[0][:, :width])
        value_rows = head_split(parts[0][:, width:])
        key_pos = first + jnp.arange(count, dtype=jnp.int32)
        key_seg = lax.dynamic_slice_in_dim(segment_row, first, count, 0)
        allowed = allowed_pairs(query_pos, query_seg, key_pos, key_seg, limit)[None]
        scores = (
            jnp.einsum("qhd,khd->hqk", queries, key_rows, preferred_element_type=jnp.float32)
            * scale
        )
        new_max = jnp.maximum(run_max, jnp.max(jnp.where(allowed, scores, NEG_BIG), axis=-1))
        shares = jnp.where(allowed, jnp.exp(scores - new_max[..., None]), 0.0)
        factor = jnp.exp(run_max - new_max)
        run_total = run_total * factor + jnp.sum(shares, axis=-1)
        update = jnp.einsum(
            "hqk,khd->qhd",
            shares.astype(jnp.bfloat16),
            value_rows,
            preferred_element_type=jnp.float32,
        )
        weighted = weighted * factor.T[:, :, None] + update
        return (new_max, run_total, weighted)

    return step


def backward_core(queries, grad_heads, log_total, delta, key_rows, value_rows, allowed):
    scale = HEAD_DIM ** (-0.5)
    scores = (
        jnp.einsum("qhd,khd->hqk", queries, key_rows, preferred_element_type=jnp.float32) * scale
    )
    soft = jnp.where(allowed[None], jnp.exp(scores - log_total[..., None]), 0.0)
    grad_soft = jnp.einsum(
        "qhd,khd->hqk", grad_heads, value_rows, preferred_element_type=jnp.float32
    )
    grad_scores = (soft * (grad_soft - delta[..., None])).astype(jnp.bfloat16)
    return (soft.astype(jnp.bfloat16), grad_scores)


def query_step(queries, grad_heads, log_total, delta, query_pos, query_seg, segment_row, limit):
    width = HEADS * HEAD_DIM
    scale = HEAD_DIM ** (-0.5)

    def step(state, parts, first):
        count = parts[0].shape[0]
        key_rows = head_split(parts[0][:, :width])
        value_rows = head_split(parts[0][:, width:])
        key_pos = first + jnp.arange(count, dtype=jnp.int32)
        key_seg = lax.dynamic_slice_in_dim(segment_row, first, count, 0)
        allowed = allowed_pairs(query_pos, query_seg, key_pos, key_seg, limit)
        soft_low, grad_scores = backward_core(
            queries, grad_heads, log_total, delta, key_rows, value_rows, allowed
        )
        grad_query = (
            jnp.einsum("hqk,khd->qhd", grad_scores, key_rows, preferred_element_type=jnp.float32)
            * scale
        )
        grad_q, grad_block = state
        grad_keys = (
            jnp.einsum("hqk,qhd->khd", grad_scores, queries, preferred_element_type=jnp.float32)
            * scale
        )
        grad_values = jnp.einsum(
            "hqk,qhd->khd", soft_low, grad_heads, preferred_element_type=jnp.float32
        )
        joined = jnp.concatenate(
            [grad_keys.reshape(count, width), grad_values.reshape(count, width)], axis=1
        )
        current = grad_block
        grad_block = current + joined
        return (grad_q + grad_query, grad_block)

    return step


def on_device(
    layer_input,
    token_ids,
    segment_ids,
    hash_table,
    first_gain,
    first_bias,
    second_gain,
    second_bias,
    w_qkv,
    w_out,
    w_up,
    w_down,
    cotangent,
):
    local_len = layer_input.shape[1]
    width = layer_input.shape[2]
    sources = lax.axis_size("exp")
    local_exp = w_up.shape[0]
    experts_total = local_exp * sources
    capacity = 2 * local_len // experts_total
    total_len = local_len * lax.axis_size("seq")
    reach_blocks = (DOC_MOST + local_len - 2) // local_len
    offset = lax.axis_index("seq") * local_len
    segment_row = segment_ids[0]
    query_pos = offset + jnp.arange(local_len, dtype=jnp.int32)
    query_seg = lax.dynamic_slice_in_dim(segment_row, offset, local_len, 0)
    inputs = layer_input[0].astype(jnp.float32)
    normed_one, scale_one = norm_rows(inputs)
    attn_in = (normed_one * first_gain + first_bias).astype(jnp.bfloat16)
    projected = jnp.dot(attn_in, w_qkv, preferred_element_type=jnp.float32).astype(jnp.bfloat16)
    queries = head_split(projected[:, :width])
    key_value = projected[:, width:]
    kv_blocks = [key_value]
    moving = key_value
    for hop_index in range(reach_blocks):
        moving = passed_along(moving, "seq", 1)
        kv_blocks.append(moving)
    state = (
        jnp.full((HEADS, local_len), NEG_BIG, jnp.float32),
        jnp.zeros((HEADS, local_len), jnp.float32),
        jnp.zeros((local_len, HEADS, HEAD_DIM), jnp.float32),
    )
    attend = forward_step(queries, query_pos, query_seg, segment_row, total_len)
    for block_index in range(reach_blocks + 1):
        state = over_blocks(
            attend, state, (kv_blocks[block_index],), offset - block_index * local_len
        )
    run_max, run_total, weighted = state
    attn_exact = (weighted / run_total.T[:, :, None]).reshape(local_len, width)
    log_total = run_max + jnp.log(run_total)
    attn_rows = attn_exact.astype(jnp.bfloat16)
    resid = inputs + jnp.dot(attn_rows, w_out, preferred_element_type=jnp.float32)
    normed_two, scale_two = norm_rows(resid)
    ffn_in = (normed_two * second_gain + second_bias).astype(jnp.bfloat16)
    choice_ids = hash_table[token_ids[0]]
    order = jnp.argsort(choice_ids, stable=True)
    places = jnp.argsort(order, stable=True)
    expert_grid = jnp.arange(experts_total, dtype=jnp.int32)
    matches = choice_ids[:, None] == expert_grid[None, :]
    counts = jnp.sum(matches.astype(jnp.int32), axis=0)
    starts = jnp.cumsum(counts) - counts
    slot_grid = jnp.arange(capacity, dtype=jnp.int32)
    gather_index = order[jnp.minimum(starts[:, None] + slot_grid[None, :], local_len - 1)]
    filled = (slot_grid[None, :] < counts[:, None])[:, :, None]
    own_start = jnp.sum(jnp.where(matches, starts[None, :], 0), axis=1)
    token_slot = choice_ids * capacity + places - own_start
    send = jnp.where(filled, ffn_in[gather_index], jnp.zeros((), jnp.bfloat16))
    received = lax.all_to_all(send, "exp", split_axis=0, concat_axis=0, tiled=True)
    grouped = received.reshape(sources, local_exp, capacity, width)
    pre_act = jnp.einsum("secd,edf->secf", grouped, w_up, preferred_element_type=jnp.float32)
    activated, gate_pullback = jax.vjp(smooth_gate, pre_act)
    hidden = activated.astype(jnp.bfloat16)
    expert_out = jnp.einsum(
        "secf,efd->secd", hidden, w_down, preferred_element_type=jnp.float32
    ).astype(jnp.bfloat16)
    returned = lax.all_to_all(
        expert_out.reshape(experts_total, capacity, width),
        "exp",
        split_axis=0,
        concat_axis=0,
        tiled=True,
    )
    ffn_rows = returned.reshape(experts_total * capacity, width)[token_slot].astype(jnp.float32)
    layer_output = (resid + ffn_rows).astype(jnp.bfloat16)
    grad_final = cotangent[0].astype(jnp.float32)
    grad_branch = grad_final.astype(jnp.bfloat16)
    grad_send = jnp.where(filled, grad_branch[gather_index], jnp.zeros((), jnp.bfloat16))
    grad_received = lax.all_to_all(
        grad_send, "exp", split_axis=0, concat_axis=0, tiled=True
    ).reshape(sources, local_exp, capacity, width)
    grad_w_down = jnp.einsum(
        "secf,secd->efd", hidden, grad_received, preferred_element_type=jnp.float32
    )
    grad_hidden = jnp.einsum(
        "secd,efd->secf", grad_received, w_down, preferred_element_type=jnp.float32
    )
    grad_pre = gate_pullback(grad_hidden)[0].astype(jnp.bfloat16)
    grad_w_up = jnp.einsum("secd,secf->edf", grouped, grad_pre, preferred_element_type=jnp.float32)
    grad_slots = jnp.einsum(
        "secf,edf->secd", grad_pre, w_up, preferred_element_type=jnp.float32
    ).astype(jnp.bfloat16)
    grad_back = lax.all_to_all(
        grad_slots.reshape(experts_total, capacity, width),
        "exp",
        split_axis=0,
        concat_axis=0,
        tiled=True,
    )
    grad_ffn_in = grad_back.reshape(experts_total * capacity, width)[token_slot].astype(jnp.float32)
    grad_second_gain = jnp.sum(grad_ffn_in * normed_two, axis=0)
    grad_second_bias = jnp.sum(grad_ffn_in, axis=0)
    grad_resid = grad_final + norm_back(grad_ffn_in * second_gain, normed_two, scale_two)
    grad_attn = grad_resid.astype(jnp.bfloat16)
    grad_w_out = jnp.einsum("cd,ce->de", attn_rows, grad_attn, preferred_element_type=jnp.float32)
    grad_out_rows = jnp.einsum(
        "ce,de->cd", grad_attn, w_out, preferred_element_type=jnp.float32
    ).astype(jnp.bfloat16)
    grad_heads = head_split(grad_out_rows)
    delta = jnp.sum(grad_heads.astype(jnp.float32) * head_split(attn_exact), axis=-1).T
    back_blocks = [key_value]
    moving = key_value
    for hop_index in range(reach_blocks):
        moving = passed_along(moving, "seq", 1)
        back_blocks.append(moving)
    grad_query = jnp.zeros((local_len, HEADS, HEAD_DIM), jnp.float32)
    block_grads = []
    for block_index in range(reach_blocks + 1):
        base = offset - block_index * local_len
        back_step = query_step(
            queries, grad_heads, log_total, delta, query_pos, query_seg, segment_row, total_len
        )
        grad_query, grad_block = over_blocks(
            back_step,
            (grad_query, jnp.zeros((local_len, 2 * width), jnp.float32)),
            (back_blocks[block_index],),
            base,
        )
        block_grads.append(grad_block)
    carried = block_grads[reach_blocks]
    for block_index in range(reach_blocks, 0, -1):
        carried = (
            passed_along(carried.astype(jnp.bfloat16), "seq", -1).astype(carried.dtype)
            + block_grads[block_index - 1]
        )
    grad_proj = jnp.concatenate([grad_query.reshape(local_len, width), carried], axis=1).astype(
        jnp.bfloat16
    )
    grad_w_qkv = jnp.einsum("cd,ce->de", attn_in, grad_proj, preferred_element_type=jnp.float32)
    grad_attn_in = jnp.einsum("ce,de->cd", grad_proj, w_qkv, preferred_element_type=jnp.float32)
    grad_first_gain = jnp.sum(grad_attn_in * normed_one, axis=0)
    grad_first_bias = jnp.sum(grad_attn_in, axis=0)
    grad_input = grad_resid + norm_back(grad_attn_in * first_gain, normed_one, scale_one)
    dense = lax.psum(
        (
            grad_w_qkv,
            grad_w_out,
            grad_first_gain,
            grad_first_bias,
            grad_second_gain,
            grad_second_bias,
        ),
        ("seq", "exp"),
    )
    expert_sums = (
        lax.psum(grad_w_up.astype(jnp.bfloat16), "seq").astype(jnp.float32),
        lax.psum(grad_w_down.astype(jnp.bfloat16), "seq").astype(jnp.float32),
    )
    return (
        layer_output[None],
        grad_input[None],
        dense[0],
        dense[1],
        dense[2],
        dense[3],
        dense[4],
        dense[5],
        expert_sums[0],
        expert_sums[1],
    )


def solution(mesh):
    in_specs = (
        P("exp", "seq", None),
        P("exp", "seq"),
        P("exp", None),
        P(),
        P(),
        P(),
        P(),
        P(),
        P(),
        P(),
        P("exp", None, None),
        P("exp", None, None),
        P("exp", "seq", None),
    )
    out_specs = (
        P("exp", "seq", None),
        P("exp", "seq", None),
        P(),
        P(),
        P(),
        P(),
        P(),
        P(),
        P("exp", None, None),
        P("exp", None, None),
    )
    return jax.shard_map(
        on_device, mesh=mesh, in_specs=in_specs, out_specs=out_specs, check_vma=False
    )
```

profile of v0, /device:TPU:0, one launch (start us, length us, event | category | flops | bytes accessed | tf_op | source)
XLA Modules:
  0.0 691.7 jit_solution(2766946564341442537)
XLA Ops:
  27.7 11.3 %gather_fusion.1 = s32[1024]{0:T(1024)} fusion(s32[512]{0:T(512)S(1)} %get-tuple-element.163, s32[1024]{0:T(1024)S(1)} %broadcast_clamp_fusion.1), kind=kCustom, calls=%fused_computation.1 | custom fusion | bytes 12288 | tf_op jit(solution)/shard_map/gather | solution.py:202
  58.6 7.0 %gather_fusion.4 = bf16[1024,768]{1,0:T(8,128)(2,1)} fusion(bf16[512,768]{1,0:T(8,128)(2,1)} %bitcast.289, s32[1024]{0:T(1024)S(1)} %broadcast_clamp_fusion), kind=kCustom, calls=%fused_computation.4 | custom fusion | bytes 3149824 | tf_op jit(solution)/shard_map/gather | solution.py:226
  65.6 8.6 %select_reduce_fusion.2 = (f32[12,512]{1,0:T(8,128)}, f32[12,512,512]{1,2,0:T(8,128)}) fusion(pred[512,512]{0,1:T(8,128)(4,1)} %get-tuple-element.239, bf16[512,12,64]{0,2,1:T(8,128)(2,1)} %bitcast.294, bf16[512,12,64]{0,2,1:T(8,128)(2,1)} %bitcast.302), kind=kOutput, calls=%fused_computation.33 | convolution fusion | flops 412084224 | bytes 14442496 | tf_op jit(solution)/shard_map/while/body/eval_jaxpr/qhd,khd->hqk/dot_general | solution.py:71
  81.5 8.6 %select_reduce_fusion.1 = (f32[12,512]{1,0:T(8,128)}, f32[12,512,512]{1,2,0:T(8,128)}) fusion(pred[512,512]{0,1:T(8,128)(4,1)} %get-tuple-element.241, bf16[512,12,64]{0,2,1:T(8,128)(2,1)} %bitcast.295, bf16[512,12,64]{0,2,1:T(8,128)(2,1)} %bitcast.300), kind=kOutput, calls=%fused_computation.31 | convolution fusion | flops 412084224 | bytes 14442496 | tf_op jit(solution)/shard_map/while/body/eval_jaxpr/qhd,khd->hqk/dot_general | solution.py:71
  97.3 8.1 %select_reduce_fusion = (f32[12,512]{1,0:T(8,128)S(1)}, f32[12,512,512]{1,2,0:T(8,128)}) fusion(pred[512,512]{0,1:T(8,128)(4,1)} %get-tuple-element.240, bf16[512,12,64]{0,2,1:T(8,128)(2,1)} %bitcast.296, bf16[512,12,64]{0,2,1:T(8,128)(2,1)} %bitcast.304), kind=kOutput, calls=%fused_computation.29 | convolution fusion | flops 412084224 | bytes 14442496 | tf_op jit(solution)/shard_map/while/body/eval_jaxpr/qhd,khd->hqk/dot_general | solution.py:71
  106.1 7.3 %fusion.13 = f32[12,512]{1,0:T(8,128)S(1)} fusion(f32[12,512,512]{1,2,0:T(8,128)} %get-tuple-element.247, f32[12,512]{1,0:T(8,128)S(1)} %get-tuple-element.210, pred[512,512]{0,1:T(8,128)(4,1)S(1)} %copy-done.19), kind=kLoop, calls=%fused_computation.36 | loop fusion | flops 12576768 | bytes 12894208 | tf_op jit(solution)/shard_map/while/body/eval_jaxpr/reduce_sum | solution.py:77
  113.4 20.8 %fusion.36 = f32[12,64,512]{2,1,0:T(8,128)} fusion(bf16[512,12,64]{0,2,1:T(8,128)(2,1)} %bitcast.324, f32[12,512,512]{1,2,0:T(8,128)} %get-tuple-element.247, f32[12,512]{1,0:T(8,128)S(1)} %get-tuple-element.210, pred[512,512]{0,1:T(8,128)(4,1)} %get-tuple-element.241), kind=kOutput, calls=%fused_computation.57 | convolution fusion | flops 415236096 | bytes 15228928 | tf_op jit(solution)/shard_map/while/body/eval_jaxpr/hqk,khd->qhd/dot_general | solution.py:78
  142.5 7.3 %fusion.15 = f32[12,512]{1,0:T(8,128)S(1)} fusion(f32[12,512,512]{1,2,0:T(8,128)} %get-tuple-element.245, f32[12,512]{1,0:T(8,128)} %get-tuple-element.196, pred[512,512]{0,1:T(8,128)(4,1)} %get-tuple-element.240), kind=kLoop, calls=%fused_computation.38 | loop fusion | flops 12576768 | bytes 12894208 | tf_op jit(solution)/shard_map/while/body/eval_jaxpr/reduce_sum | solution.py:77
  150.0 8.8 %fusion.158 = (bf16[512,12,64]{0,2,1:T(8,128)(2,1)S(1)}, f32[512,12,64]{0,2,1:T(8,128)}) fusion(f32[512,12]{0,1:T(8,128)S(1)} %get-tuple-element.194, bf16[512,12,64]{0,2,1:T(8,128)(2,1)S(1)} %bitcast.326, f32[12,512,512]{1,2,0:T(8,128)} %get-tuple-element.245, f32[12,512]{1,0:T(8,128)S(1)} %copy-done.37, pred[512,512]{0,1:T(8,128)(4,1)S(1)} %copy-done.21, ...), kind=kOutput, calls=%fused_computation.216 | convolution fusion | flops 417988608 | bytes 19259392 | tf_op jit(solution)/shard_map/while/body/eval_jaxpr/hqk,khd->qhd/dot_general | solution.py:78
  162.6 7.0 %gather_fusion.2 = bf16[1024,768]{1,0:T(8,128)(2,1)} fusion(bf16[512,768]{1,0:T(8,128)(2,1)} %add_convert_fusion.1, s32[1024]{0:T(1024)} %copy-done.44), kind=kCustom, calls=%fused_computation.2 | custom fusion | bytes 3149824 | tf_op jit(solution)/shard_map/gather | solution.py:206
  173.5 4.9 all-to-all-start
  186.3 28.2 %all-to-all-done = bf16[4,256,768]{2,1,0:T(8,128)(2,1)} async-done(((bf16[4,256,768]{2,1,0:T(8,128)(2,1)}), bf16[4,256,768]{2,1,0:T(8,128)(2,1)}, u32[]{:S(2)}, u32[]{:S(2)}) %all-to-all-start) | async-done | bytes 1572896 | tf_op jit(solution)/shard_map/all_to_all | solution.py:207
  218.9 7.4 %fusion.54 = f32[4,256,3072]{2,1,0:T(8,128)S(1)} fusion(bf16[4,256,768]{2,1,0:T(8,128)(2,1)} %all-to-all-done, bf16[1,768,3072]{2,1,0:T(8,128)(2,1)} %param.23), kind=kOutput, calls=%fused_computation.69 | convolution fusion | flops 4831838208 | bytes 18874368 | tf_op jit(solution)/shard_map/secd,edf->secf/dot_general | solution.py:209
  230.7 10.8 %fusion.77 = bf16[4,256,768]{2,1,0:T(8,128)(2,1)} fusion(bf16[1,3072,768]{2,1,0:T(8,128)(2,1)} %param.24, f32[4,256,3072]{2,1,0:T(8,128)S(1)} %fusion.54), kind=kOutput, calls=%fused_computation.95 | convolution fusion | flops 4860936192 | bytes 18874368 | tf_op jit(solution)/shard_map/secf,efd->secd/dot_general | solution.py:212
  241.5 13.9 %all-to-all-done.2 = bf16[4,256,768]{2,1,0:T(8,128)(2,1)} async-done(((bf16[4,256,768]{2,1,0:T(8,128)(2,1)}), bf16[4,256,768]{2,1,0:T(8,128)(2,1)}, u32[]{:S(2)}, u32[]{:S(2)}) %all-to-all-start.2) | async-done | bytes 1572896 | tf_op jit(solution)/shard_map/all_to_all | solution.py:227
  260.2 15.3 %fusion.6 = bf16[4,1,256,3072]{3,2,0,1:T(8,128)(2,1)S(1)} fusion(f32[4,256,3072]{2,1,0:T(8,128)} %copy-done.64, bf16[4,256,768]{2,1,0:T(8,128)(2,1)} %all-to-all-done.2, bf16[1,3072,768]{2,1,0:T(8,128)(2,1)} %param.24), kind=kOutput, calls=%fused_computation.14 | convolution fusion | flops 4894752768 | bytes 25165824 | tf_op jit(solution)/shard_map/secd,efd->secf/dot_general | solution.py:233
  275.5 8.5 %fusion.82 = bf16[4,256,768]{2,1,0:T(8,128)(2,1)} fusion(bf16[1,768,3072]{2,1,0:T(8,128)(2,1)} %param.23, bf16[4,1,256,3072]{3,2,0,1:T(8,128)(2,1)S(1)} %fusion.6), kind=kOutput, calls=%fused_computation.96 | convolution fusion | flops 4832624640 | bytes 12582912 | tf_op jit(solution)/shard_map/secf,edf->secd/dot_general | solution.py:238
  284.1 8.2 %fusion.56 = bf16[1,768,3072]{2,1,0:T(8,128)(2,1)} fusion(bf16[4,256,768]{2,1,0:T(8,128)(2,1)} %all-to-all-done, bf16[4,1,256,3072]{3,2,0,1:T(8,128)(2,1)S(1)} %fusion.6), kind=kOutput, calls=%fused_computation.71 | convolution fusion | flops 4834197504 | bytes 12582912 | tf_op jit(solution)/shard_map/secd,secf->edf/dot_general | solution.py:237
  301.1 12.0 %fusion.59 = bf16[1,3072,768]{2,1,0:T(8,128)(2,1)} fusion(bf16[4,256,768]{2,1,0:T(8,128)(2,1)} %all-to-all-done.2, f32[4,256,3072]{2,1,0:T(8,128)} %copy-done.64), kind=kOutput, calls=%fused_computation.72 | convolution fusion | flops 4862509056 | bytes 18874368 | tf_op jit(solution)/shard_map/secf,secd->efd/dot_general | solution.py:230
  318.1 19.5 %all-to-all-done.3 = bf16[4,256,768]{2,1,0:T(8,128)(2,1)} async-done(((bf16[4,256,768]{2,1,0:T(8,128)(2,1)}), bf16[4,256,768]{2,1,0:T(8,128)(2,1)}, u32[]{:S(2)}, u32[]{:S(2)}) %all-to-all-start.3) | async-done | bytes 1572896 | tf_op jit(solution)/shard_map/all_to_all | solution.py:241
  356.2 8.6 %fusion.110 = bf16[12,64,512]{2,1,0:T(8,128)(2,1)} fusion(bf16[512,12,64]{0,2,1:T(8,128)(2,1)} %bitcast.311, f32[12,512,512]{1,2,0:T(8,128)} %get-tuple-element.245, f32[12,512]{1,0:T(8,128)} %log_add_fusion, pred[512,512]{0,1:T(8,128)(4,1)} %get-tuple-element.240), kind=kOutput, calls=%fused_computation.132 | convolution fusion | flops 415629312 | bytes 14442496 | tf_op jit(solution)/shard_map/while/body/eval_jaxpr/hqk,qhd->khd/dot_general | solution.py:126
  364.8 7.8 %multiply_convert_fusion = bf16[12,512,512]{1,2,0:T(8,128)(2,1)S(1)} fusion(f32[12,512,512]{1,2,0:T(8,128)} %get-tuple-element.245, f32[12,512]{1,0:T(8,128)S(1)} %bitcast.331, f32[12,512]{1,0:T(8,128)S(1)} %copy-done.47, pred[512,512]{0,1:T(8,128)(4,1)S(1)} %copy-done.22, bf16[512,12,64]{0,2,1:T(8,128)(2,1)S(1)} %bitcast.312, ...), kind=kOutput, calls=%fused_computation.22 | convolution fusion | flops 421527552 | bytes 20758528 | tf_op jit(solution)/shard_map/while/body/eval_jaxpr/qhd,khd->hqk/dot_general | solution.py:96
  372.7 7.6 %multiply_convert_fusion.2 = bf16[12,512,512]{1,2,0:T(8,128)(2,1)S(1)} fusion(f32[12,512,512]{1,2,0:T(8,128)} %get-tuple-element.262, f32[12,512]{1,0:T(8,128)S(1)} %bitcast.332, f32[12,512]{1,0:T(8,128)S(1)} %copy-done.47, pred[512,512]{0,1:T(8,128)(4,1)} %get-tuple-element.239, bf16[512,12,64]{0,2,1:T(8,128)(2,1)S(1)} %bitcast.313, ...), kind=kOutput, calls=%fused_computation.26 | convolution fusion | flops 421527552 | bytes 20758528 | tf_op jit(solution)/shard_map/while/body/eval_jaxpr/qhd,khd->hqk/dot_general | solution.py:96
  385.8 8.0 %multiply_convert_fusion.1 = bf16[12,512,512]{1,2,0:T(8,128)(2,1)S(1)} fusion(f32[12,512,512]{1,2,0:T(8,128)} %get-tuple-element.247, f32[12,512]{1,0:T(8,128)S(1)} %bitcast.333, f32[12,512]{1,0:T(8,128)S(1)} %copy-done.47, pred[512,512]{0,1:T(8,128)(4,1)} %get-tuple-element.241, bf16[512,12,64]{0,2,1:T(8,128)(2,1)S(1)} %bitcast.314, ...), kind=kOutput, calls=%fused_computation.24 | convolution fusion | flops 421527552 | bytes 20758528 | tf_op jit(solution)/shard_map/while/body/eval_jaxpr/qhd,khd->hqk/dot_general | solution.py:96
  404.0 6.1 fusion.30
  423.5 14.7 %collective-permute-done.3 = bf16[512,1536]{0,1:T(8,128)(2,1)} collective-permute-done((bf16[512,1536]{0,1:T(8,128)(2,1)}, bf16[512,1536]{0,1:T(8,128)(2,1)}, u32[]{:S(2)}, u32[]{:S(2)}) %collective-permute-start.3) | collective-permute-done | bytes 1572896 | tf_op jit(solution)/shard_map/ppermute | solution.py:17
  441.4 5.3 fusion.106
  446.7 23.3 %all-reduce.8.cloned.1.call-done = (bf16[1,768,3072]{2,1,0:T(8,128)(2,1)}, bf16[1,3072,768]{2,1,0:T(8,128)(2,1)}) async-done(((bf16[1,768,3072]{2,1,0:T(8,128)(2,1)}, bf16[1,3072,768]{2,1,0:T(8,128)(2,1)}), (bf16[1,768,3072]{2,1,0:T(8,128)(2,1)}, bf16[1,3072,768]{2,1,0:T(8,128)(2,1)})) %all-reduce.8.cloned.1.call-update) | async-done | bytes 9437200 | tf_op jit(solution)/shard_map/psum | solution.py:304
  470.0 7.5 %convert_element_type.162 = f32[1,768,3072]{2,1,0:T(8,128)} convert(bf16[1,768,3072]{2,1,0:T(8,128)(2,1)} %get-tuple-element.192) | non-fusion elementwise | flops 2359296 | bytes 14155776 | tf_op jit(solution)/shard_map/convert_element_type | solution.py:304
  486.2 55.8 %all-reduce = (f32[768]{0:T(1024)}, f32[768]{0:T(1024)}, f32[768]{0:T(1024)}, f32[768]{0:T(1024)}) all-reduce(f32[768]{0:T(1024)} %get-tuple-element.167, f32[768]{0:T(1024)} %get-tuple-element.170, f32[768]{0:T(1024)S(1)} %get-tuple-element.165, f32[768]{0:T(1024)S(1)} %copy-done.50), channel_id=1, replica_groups=mesh['seq'=8,'exp'=4] {'seq','exp'}, use_global_device_ids=true, to_apply=%region_23.24 | all-reduce | flops 3072 | bytes 24576 | tf_op jit(solution)/shard_map/psum | solution.py:292
  547.3 129.1 %all-reduce.6.cloned.1.call-done = (f32[768,2304]{1,0:T(8,128)}, f32[768,768]{1,0:T(8,128)}) async-done(((f32[768,2304]{1,0:T(8,128)}, f32[768,768]{1,0:T(8,128)}), (f32[768,2304]{1,0:T(8,128)}, f32[768,768]{1,0:T(8,128)})) %all-reduce.6.cloned.1.call-update) | async-done | bytes 9437200 | tf_op jit(solution)/shard_map/psum | solution.py:292
  676.4 6.6 copy.132
  (239 shorter events, 172.4 us)
Async XLA Ops:
  10.2 9.6 %copy-start.57 = (s32[1,512]{1,0:T(1,128)S(1)}, s32[1,512]{1,0:T(1,128)}, u32[]{:S(2)}) copy-start(s32[1,512]{1,0:T(1,128)} %param.14) | copy-start | bytes 6148
  16.2 29.7 %collective-permute-start = (bf16[512,1536]{1,0:T(8,128)(2,1)}, bf16[512,1536]{1,0:T(8,128)(2,1)}, u32[]{:S(2)}, u32[]{:S(2)}) collective-permute-start(bf16[512,1536]{1,0:T(8,128)(2,1)} %slice.67), channel_id=1, source_target_pairs={{0,4},{4,8},{8,12},{12,16},{16,20},{20,24},{24,28},{1,5},{5,9},{9,... | collective-permute-start | bytes 4718600 | tf_op jit(solution)/shard_map/ppermute | solution.py:17
  40.5 18.1 %copy-start.44 = (s32[1024]{0:T(1024)}, s32[1024]{0:T(1024)S(1)}, u32[]{:S(2)}) copy-start(s32[1024]{0:T(1024)S(1)} %broadcast_clamp_fusion) | copy-start | bytes 12292
  45.9 44.2 %collective-permute-start.1 = (bf16[512,1536]{1,0:T(8,128)(2,1)}, bf16[512,1536]{1,0:T(8,128)(2,1)}, u32[]{:S(2)}, u32[]{:S(2)}) collective-permute-start(bf16[512,1536]{1,0:T(8,128)(2,1)} %collective-permute-done), channel_id=1, source_target_pairs={{0,4},{4,8},{8,12},{12,16},{16,20},{20,24},{24,28},{1,5},{5,9},{9,... | collective-permute-start | bytes 4718600 | tf_op jit(solution)/shard_map/ppermute | solution.py:17
  97.3 8.8 %copy-start.19 = (pred[512,512]{0,1:T(8,128)(4,1)S(1)}, pred[512,512]{0,1:T(8,128)(4,1)}, u32[]{:S(2)}) copy-start(pred[512,512]{0,1:T(8,128)(4,1)} %get-tuple-element.241) | copy-start | bytes 786436
  106.1 28.1 %slice-start = ((s8[12582912]{0:T(1024)(128)(4,1)}), s8[4194304]{0:T(1024)(128)(4,1)S(1)}, s32[]{:S(2)}) async-start(s8[12582912]{0:T(1024)(128)(4,1)} %bitcast.290), calls=%async_computation.6 | async-start | bytes 8388608
  106.1 28.1 %slice-start.1 = ((s8[12582912]{0:T(1024)(128)(4,1)}), s8[4194304]{0:T(1024)(128)(4,1)S(1)}, s32[]{:S(2)}) async-start(s8[12582912]{0:T(1024)(128)(4,1)} %bitcast.290), calls=%async_computation.7 | async-start | bytes 8388608
  113.4 36.4 %copy-start.34 = (f32[12,512]{1,0:T(8,128)}, f32[12,512]{1,0:T(8,128)S(1)}, u32[]{:S(2)}) copy-start(f32[12,512]{1,0:T(8,128)S(1)} %fusion.13) | copy-start | bytes 73732
  113.4 20.8 %slice-start.2 = ((s8[12582912]{0:T(1024)(128)(4,1)}), s8[4194304]{0:T(1024)(128)(4,1)S(1)}, s32[]{:S(2)}) async-start(s8[12582912]{0:T(1024)(128)(4,1)} %bitcast.290), calls=%async_computation.8 | async-start | bytes 8388608
  137.8 12.1 %copy-start.35 = (f32[12,512]{1,0:T(8,128)}, f32[12,512]{1,0:T(8,128)S(1)}, u32[]{:S(2)}) copy-start(f32[12,512]{1,0:T(8,128)S(1)} %fusion.11) | copy-start | bytes 73732
  149.9 8.9 %copy-start.36 = (f32[12,512]{1,0:T(8,128)}, f32[12,512]{1,0:T(8,128)S(1)}, u32[]{:S(2)}) copy-start(f32[12,512]{1,0:T(8,128)S(1)} %fusion.15) | copy-start | bytes 73732
  150.0 8.8 %copy-start.10 = (bf16[1,512,768]{2,1,0:T(8,128)(2,1)S(1)}, bf16[1,512,768]{2,1,0:T(8,128)(2,1)}, u32[]{:S(2)}) copy-start(bf16[1,512,768]{2,1,0:T(8,128)(2,1)} %param.13) | copy-start | bytes 2359300
  150.0 8.8 %copy-start.59 = (bf16[768,768]{1,0:T(8,128)(2,1)S(1)}, bf16[768,768]{1,0:T(8,128)(2,1)}, u32[]{:S(2)}) copy-start(bf16[768,768]{1,0:T(8,128)(2,1)} %param.22) | copy-start | bytes 3538948
  173.5 41.0 %all-to-all-start = ((bf16[4,256,768]{2,1,0:T(8,128)(2,1)}), bf16[4,256,768]{2,1,0:T(8,128)(2,1)}, u32[]{:S(2)}, u32[]{:S(2)}) async-start(bf16[4,256,768]{2,1,0:T(8,128)(2,1)} %get-tuple-element.243), calls=%async_computation | async-start | bytes 3145728 | tf_op jit(solution)/shard_map/all_to_all | solution.py:207
  214.5 40.9 %all-to-all-start.2 = ((bf16[4,256,768]{2,1,0:T(8,128)(2,1)}), bf16[4,256,768]{2,1,0:T(8,128)(2,1)}, u32[]{:S(2)}, u32[]{:S(2)}) async-start(bf16[4,256,768]{2,1,0:T(8,128)(2,1)} %get-tuple-element.242), calls=%async_computation.2 | async-start | bytes 3145728 | tf_op jit(solution)/shard_map/all_to_all | solution.py:227
  255.4 41.3 %all-to-all-start.1 = ((bf16[4,256,768]{2,1,0:T(8,128)(2,1)}), bf16[4,256,768]{2,1,0:T(8,128)(2,1)}, u32[]{:S(2)}, u32[]{:S(2)}) async-start(bf16[4,256,768]{2,1,0:T(8,128)(2,1)} %fusion.77), calls=%async_computation.1 | async-start | bytes 3145728 | tf_op jit(solution)/shard_map/all_to_all | solution.py:215
  296.7 40.9 %all-to-all-start.3 = ((bf16[4,256,768]{2,1,0:T(8,128)(2,1)}), bf16[4,256,768]{2,1,0:T(8,128)(2,1)}, u32[]{:S(2)}, u32[]{:S(2)}) async-start(bf16[4,256,768]{2,1,0:T(8,128)(2,1)} %fusion.82), calls=%async_computation.3 | async-start | bytes 3145728 | tf_op jit(solution)/shard_map/all_to_all | solution.py:241
  301.1 169.0 %all-reduce.8.cloned.1.call-start = ((), (), s32[]{:S(2)}) async-start(), calls=%async_computation.5 | async-start | bytes 18874368 | tf_op jit(solution)/shard_map/psum | solution.py:304
  313.2 363.2 %all-reduce.6.cloned.1.call-start = ((), (), s32[]{:S(2)}) async-start(), calls=%async_computation.4 | async-start | bytes 18874368 | tf_op jit(solution)/shard_map/psum | solution.py:292
  318.1 24.2 %copy-start.46 = (f32[512]{0:T(512)S(1)}, f32[512]{0:T(512)}, u32[]{:S(2)}) copy-start(f32[512]{0:T(512)} %copy-done.45) | copy-start | bytes 6148
  356.2 8.6 %copy-start.17 = (bf16[512,768]{0,1:T(8,128)(2,1)S(1)}, bf16[512,768]{0,1:T(8,128)(2,1)}, u32[]{:S(2)}) copy-start(bf16[512,768]{0,1:T(8,128)(2,1)} %copy.94) | copy-start | bytes 2359300
  397.1 13.0 %collective-permute-start.2 = (bf16[512,1536]{0,1:T(8,128)(2,1)}, bf16[512,1536]{0,1:T(8,128)(2,1)}, u32[]{:S(2)}, u32[]{:S(2)}) collective-permute-start(bf16[512,1536]{0,1:T(8,128)(2,1)} %pad_maximum_fusion.1), channel_id=1, source_target_pairs={{4,0},{8,4},{12,8},{16,12},{20,16},{24,20},{28,24},{5,1},{9,5},{13... | collective-permute-start | bytes 4718600 | tf_op jit(solution)/shard_map/ppermute | solution.py:17
  404.0 15.7 %slice-start.3 = ((s8[12582912]{0:T(1024)(128)(4,1)}), s8[4194304]{0:T(1024)(128)(4,1)S(1)}, s32[]{:S(2)}) async-start(s8[12582912]{0:T(1024)(128)(4,1)} %bitcast.292), calls=%async_computation.9 | async-start | bytes 8388608
  404.0 15.7 %slice-start.4 = ((s8[12582912]{0:T(1024)(128)(4,1)}), s8[4194304]{0:T(1024)(128)(4,1)S(1)}, s32[]{:S(2)}) async-start(s8[12582912]{0:T(1024)(128)(4,1)} %bitcast.292), calls=%async_computation.10 | async-start | bytes 8388608
  413.6 24.5 %collective-permute-start.3 = (bf16[512,1536]{0,1:T(8,128)(2,1)}, bf16[512,1536]{0,1:T(8,128)(2,1)}, u32[]{:S(2)}, u32[]{:S(2)}) collective-permute-start(bf16[512,1536]{0,1:T(8,128)(2,1)} %fusion.64), channel_id=1, source_target_pairs={{4,0},{8,4},{12,8},{16,12},{20,16},{24,20},{28,24},{5,1},{9,5},{13... | collective-permute-start | bytes 4718600 | tf_op jit(solution)/shard_map/ppermute | solution.py:17
  419.8 18.4 %copy-start.14 = (f32[12,64,512]{2,1,0:T(8,128)S(1)}, f32[12,64,512]{2,1,0:T(8,128)}, u32[]{:S(2)}) copy-start(f32[12,64,512]{2,1,0:T(8,128)} %convolution_multiply_fusion) | copy-start | bytes 4718596
  423.4 17.9 %copy-start.11 = (bf16[1,512,768]{2,1,0:T(8,128)(2,1)S(1)}, bf16[1,512,768]{2,1,0:T(8,128)(2,1)}, u32[]{:S(2)}) copy-start(bf16[1,512,768]{2,1,0:T(8,128)(2,1)} %param.13) | copy-start | bytes 2359300
  423.4 17.9 %copy-start.31 = (bf16[12,64,512]{2,1,0:T(8,128)(2,1)S(1)}, bf16[12,64,512]{2,1,0:T(8,128)(2,1)}, u32[]{:S(2)}) copy-start(bf16[12,64,512]{2,1,0:T(8,128)(2,1)} %multiply_convert_fusion.4) | copy-start | bytes 2359300
  423.4 17.9 %copy-start.49 = (f32[512]{0:T(512)S(1)}, f32[512]{0:T(512)}, u32[]{:S(2)}) copy-start(f32[512]{0:T(512)} %copy-done.48) | copy-start | bytes 6148
  423.4 17.9 %copy-start.52 = (f32[512]{0:T(512)S(1)}, f32[512]{0:T(512)}, u32[]{:S(2)}) copy-start(f32[512]{0:T(512)} %copy-done.51) | copy-start | bytes 6148
  423.4 17.9 %copy-start.54 = (f32[768]{0:T(1024)S(1)}, f32[768]{0:T(1024)}, u32[]{:S(2)}) copy-start(f32[768]{0:T(1024)} %param.17) | copy-start | bytes 9220
  423.4 17.9 %copy-start.61 = (f32[768]{0:T(1024)S(1)}, f32[768]{0:T(1024)}, u32[]{:S(2)}) copy-start(f32[768]{0:T(1024)} %param.18) | copy-start | bytes 9220
  (49 other events, 252.8 us)
Sparse Core Ops, SparseCore 0:
  313.3 156.6 all-reduce.7
  477.5 198.8 all-reduce.5
where the time goes:
time: 699 us; the launch traced here: 692 us
  waiting for transfers between devices  233 us (33%)
  matrix products  196 us (28%)
  local copies, waits for them, and re-layouts  86.4 us (12%)
  other arithmetic  74.9 us (11%)
  blocking collectives  55.8 us (8%)
  starting transfers between devices  29.9 us (4%)
  between operations  15.3 us (2%)
    psum x1, waiting for transfers between devices, on_device(): lax.psum((grad_w_qkv, grad_w_out, grad_first_gain, grad_first_bias, grad_...  129 us
    psum x1, blocking collectives, on_device(): lax.psum((grad_w_qkv, grad_w_out, grad_first_gain, grad_first_bias, grad_...  55.8 us
    dot_general x3, matrix products, step(): jnp.einsum('hqk,khd->qhd', shares.astype(jnp.bfloat16), value_rows, prefe...  34.3 us
    all_to_all x1, waiting for transfers between devices, on_device(): lax.all_to_all(send, 'exp', split_axis=0, concat_axis=0, tiled=True)  28.2 us
    dot_general x3, matrix products, step(): jnp.einsum('qhd,khd->hqk', queries, key_rows, preferred_element_type=jnp....  25.3 us
    dot_general x3, matrix products, backward_core(): jnp.einsum('qhd,khd->hqk', grad_heads, value_rows, preferred_element_type...  23.4 us
    psum x1, waiting for transfers between devices, on_device(): lax.psum(grad_w_up.astype(jnp.bfloat16), 'seq').astype(jnp.float32)  23.3 us
    all_to_all x1, waiting for transfers between devices, on_device(): lax.all_to_all(grad_slots.reshape(experts_total, capacity, width), 'exp',...  19.5 us
  transfers between devices with their start and end apart: 10, of which 7 were waited for; matrix products, arithmetic and copies ran while one was open for 36% of the time, Pallas kernels for 0%

commit v1 on v0

--- a/solution.py
+++ b/solution.py
@@ -9,6 +9,29 @@
 DOC_MOST = 1024
 NEG_BIG = -1e30
 EPSILON = 1e-05
+
+
+def link_plate(patch, mesh_ax, array_dim, d_out):
+    upper, state_now = (lax.psum(1, mesh_ax), lax.axis_index(mesh_ax))
+    found_now = list(patch.shape)
+    work_now = patch.shape[array_dim] // upper
+    found_now[array_dim] = work_now
+    passed = found_now[d_out]
+    found_now[d_out] = passed * upper
+    u = 0
+    shaped = jnp.zeros(found_now, patch.dtype)
+    while u < upper:
+        aux = lax.dynamic_slice_in_dim(patch, (state_now ^ u) * work_now, work_now, axis=array_dim)
+        if u:
+            shelf = []
+            d = 0
+            while d < upper:
+                shelf.append((d, d ^ u))
+                d += 1
+            aux = lax.ppermute(aux, mesh_ax, shelf)
+        shaped = lax.dynamic_update_slice_in_dim(shaped, aux, (state_now ^ u) * passed, axis=d_out)
+        u += 1
+    return shaped
 
 
 def passed_along(block, axis, distance):
@@ -204,7 +227,7 @@
     own_start = jnp.sum(jnp.where(matches, starts[None, :], 0), axis=1)
     token_slot = choice_ids * capacity + places - own_start
     send = jnp.where(filled, ffn_in[gather_index], jnp.zeros((), jnp.bfloat16))
-    received = lax.all_to_all(send, "exp", split_axis=0, concat_axis=0, tiled=True)
+    received = link_plate(send, "exp", 0, 0)
     grouped = received.reshape(sources, local_exp, capacity, width)
     pre_act = jnp.einsum("secd,edf->secf", grouped, w_up, preferred_element_type=jnp.float32)
     activated, gate_pullback = jax.vjp(smooth_gate, pre_act)

time: 699 us -> 711 us (1.017)
  starting transfers between devices: 29.9 us -> 48.5 us
    ppermute x0 -> x3, waiting for transfers between devices: none -> 37.1 us  [link_plate(): aux = lax.ppermute(aux, mesh_ax, shelf)]
    all_to_all x1 -> x0, waiting for transfers between devices: 28.2 us -> none  [on_device(): lax.all_to_all(send, 'exp', split_axis=0, concat_axis=0, tiled=True)]
    all_to_all x1, starting transfers between devices: 4.78 us -> 20.2 us  [on_device(): lax.all_to_all(expert_out.reshape(experts_total, capacity, width), 'exp',...]
    all_to_all x1, waiting for transfers between devices: 13.9 us -> 0.01 us  [on_device(): lax.all_to_all(grad_send, 'exp', split_axis=0, concat_axis=0, tiled=True)]
    ppermute x0 -> x3, starting transfers between devices: none -> 8 us  [link_plate(): aux = lax.ppermute(aux, mesh_ax, shelf)]
    unnamed x146 -> x156, local copies, waits for them, and re-layouts: 18.2 us -> 19.3 us
  transfers between devices with their start and end apart: 10 -> 12, of which waited for: 7 -> 8; matrix products, arithmetic and copies ran while one was open for 36% -> 35% of each run, Pallas kernels for 0% -> 0%
where the time goes in v1:
time: 711 us; the launch traced here: 704 us
  waiting for transfers between devices  229 us (32%)
  matrix products  195 us (27%)
  local copies, waits for them, and re-layouts  87 us (12%)
  other arithmetic  72.8 us (10%)
  blocking collectives  56.7 us (8%)
  starting transfers between devices  48.5 us (7%)
  between operations  15.4 us (2%)
    psum x1, waiting for transfers between devices, on_device(): lax.psum((grad_w_qkv, grad_w_out, grad_first_gain, grad_first_bias, grad_...  129 us
    psum x1, blocking collectives, on_device(): lax.psum((grad_w_qkv, grad_w_out, grad_first_gain, grad_first_bias, grad_...  56.7 us
    ppermute x3, waiting for transfers between devices, link_plate(): aux = lax.ppermute(aux, mesh_ax, shelf)  37.1 us
    dot_general x3, matrix products, step(): jnp.einsum('hqk,khd->qhd', shares.astype(jnp.bfloat16), value_rows, prefe...  34.4 us
    dot_general x3, matrix products, step(): jnp.einsum('qhd,khd->hqk', queries, key_rows, preferred_element_type=jnp....  25.2 us
    dot_general x3, matrix products, backward_core(): jnp.einsum('qhd,khd->hqk', grad_heads, value_rows, preferred_element_type...  23.4 us
    psum x1, waiting for transfers between devices, on_device(): lax.psum(grad_w_up.astype(jnp.bfloat16), 'seq').astype(jnp.float32)  20.3 us
    all_to_all x1, waiting for transfers between devices, on_device(): lax.all_to_all(grad_slots.reshape(experts_total, capacity, width), 'exp',...  20.3 us
  transfers between devices with their start and end apart: 12, of which 8 were waited for; matrix products, arithmetic and copies ran while one was open for 35% of the time, Pallas kernels for 0%

profile of v1, /device:TPU:0, one launch (start us, length us, event | category | flops | bytes accessed | tf_op | source)
XLA Modules:
  0.0 704.1 jit_solution(4435883542559779204)
XLA Ops:
  31.5 6.9 gather_fusion.1
  48.4 6.8 gather_fusion.4
  64.9 8.5 %select_reduce_fusion.2 = (f32[12,512]{1,0:T(8,128)}, f32[12,512,512]{1,2,0:T(8,128)}) fusion(pred[512,512]{0,1:T(8,128)(4,1)S(1)} %get-tuple-element.243, bf16[512,12,64]{0,2,1:T(8,128)(2,1)} %bitcast.294, bf16[512,12,64]{0,2,1:T(8,128)(2,1)} %bitcast.300), kind=kOutput, calls=%fused_computation.33 | convolution fusion | flops 412084224 | bytes 14442496 | tf_op jit(solution)/shard_map/while/body/eval_jaxpr/qhd,khd->hqk/dot_general | solution.py:94
  80.6 8.6 %select_reduce_fusion.1 = (f32[12,512]{1,0:T(8,128)}, f32[12,512,512]{1,2,0:T(8,128)}) fusion(pred[512,512]{0,1:T(8,128)(4,1)} %get-tuple-element.245, bf16[512,12,64]{0,2,1:T(8,128)(2,1)} %bitcast.295, bf16[512,12,64]{0,2,1:T(8,128)(2,1)} %bitcast.302), kind=kOutput, calls=%fused_computation.31 | convolution fusion | flops 412084224 | bytes 14442496 | tf_op jit(solution)/shard_map/while/body/eval_jaxpr/qhd,khd->hqk/dot_general | solution.py:94
  96.5 8.1 %select_reduce_fusion = (f32[12,512]{1,0:T(8,128)S(1)}, f32[12,512,512]{1,2,0:T(8,128)}) fusion(pred[512,512]{0,1:T(8,128)(4,1)} %get-tuple-element.244, bf16[512,12,64]{0,2,1:T(8,128)(2,1)} %bitcast.296, bf16[512,12,64]{0,2,1:T(8,128)(2,1)} %bitcast.304), kind=kOutput, calls=%fused_computation.29 | convolution fusion | flops 412084224 | bytes 14442496 | tf_op jit(solution)/shard_map/while/body/eval_jaxpr/qhd,khd->hqk/dot_general | solution.py:94
  105.2 7.3 %fusion.13 = f32[12,512]{1,0:T(8,128)S(1)} fusion(f32[12,512,512]{1,2,0:T(8,128)} %get-tuple-element.264, f32[12,512]{1,0:T(8,128)S(1)} %get-tuple-element.210, pred[512,512]{0,1:T(8,128)(4,1)S(1)} %copy-done.20), kind=kLoop, calls=%fused_computation.36 | loop fusion | flops 12576768 | bytes 12894208 | tf_op jit(solution)/shard_map/while/body/eval_jaxpr/reduce_sum | solution.py:100
  112.6 20.9 %fusion.36 = f32[12,64,512]{2,1,0:T(8,128)} fusion(bf16[512,12,64]{0,2,1:T(8,128)(2,1)} %bitcast.324, f32[12,512,512]{1,2,0:T(8,128)} %get-tuple-element.264, f32[12,512]{1,0:T(8,128)S(1)} %get-tuple-element.210, pred[512,512]{0,1:T(8,128)(4,1)} %get-tuple-element.245), kind=kOutput, calls=%fused_computation.57 | convolution fusion | flops 415236096 | bytes 15228928 | tf_op jit(solution)/shard_map/while/body/eval_jaxpr/hqk,khd->qhd/dot_general | solution.py:101
  141.8 7.3 %fusion.15 = f32[12,512]{1,0:T(8,128)S(1)} fusion(f32[12,512,512]{1,2,0:T(8,128)} %get-tuple-element.262, f32[12,512]{1,0:T(8,128)} %get-tuple-element.196, pred[512,512]{0,1:T(8,128)(4,1)} %get-tuple-element.244), kind=kLoop, calls=%fused_computation.38 | loop fusion | flops 12576768 | bytes 12894208 | tf_op jit(solution)/shard_map/while/body/eval_jaxpr/reduce_sum | solution.py:100
  149.3 8.8 %fusion.158 = (bf16[512,12,64]{0,2,1:T(8,128)(2,1)S(1)}, f32[512,12,64]{0,2,1:T(8,128)}) fusion(f32[512,12]{0,1:T(8,128)S(1)} %get-tuple-element.194, bf16[512,12,64]{0,2,1:T(8,128)(2,1)S(1)} %bitcast.326, f32[12,512,512]{1,2,0:T(8,128)} %get-tuple-element.262, f32[12,512]{1,0:T(8,128)S(1)} %copy-done.40, pred[512,512]{0,1:T(8,128)(4,1)S(1)} %copy-done.22, ...), kind=kOutput, calls=%fused_computation.223 | convolution fusion | flops 417988608 | bytes 19259392 | tf_op jit(solution)/shard_map/while/body/eval_jaxpr/hqk,khd->qhd/dot_general | solution.py:101
  161.9 6.8 gather_fusion.2
  188.2 6.8 collective-permute-done.2
  196.8 9.0 %collective-permute-done.3 = bf16[1,256,768]{2,1,0:T(8,128)(2,1)} collective-permute-done((bf16[1,256,768]{2,1,0:T(8,128)(2,1)}, bf16[1,256,768]{2,1,0:T(8,128)(2,1)}, u32[]{:S(2)}, u32[]{:S(2)}) %collective-permute-start.3) | collective-permute-done | bytes 393248 | tf_op jit(solution)/shard_map/ppermute | solution.py:31
  207.6 21.2 %collective-permute-done.4 = bf16[1,256,768]{2,1,0:T(8,128)(2,1)S(1)} collective-permute-done((bf16[1,256,768]{2,1,0:T(8,128)(2,1)}, bf16[1,256,768]{2,1,0:T(8,128)(2,1)S(1)}, u32[]{:S(2)}, u32[]{:S(2)}) %collective-permute-start.4) | collective-permute-done | bytes 393248 | tf_op jit(solution)/shard_map/ppermute | solution.py:31
  229.6 7.3 %fusion.54 = f32[4,256,3072]{2,1,0:T(8,128)S(1)} fusion(bf16[4,256,768]{2,1,0:T(8,128)(2,1)} %constant_dynamic-update-slice_fusion, bf16[1,768,3072]{2,1,0:T(8,128)(2,1)} %param.23), kind=kOutput, calls=%fused_computation.69 | convolution fusion | flops 4831838208 | bytes 18874368 | tf_op jit(solution)/shard_map/secd,edf->secf/dot_general | solution.py:232
  241.4 10.8 %fusion.77 = bf16[4,256,768]{2,1,0:T(8,128)(2,1)} fusion(bf16[1,3072,768]{2,1,0:T(8,128)(2,1)} %param.24, f32[4,256,3072]{2,1,0:T(8,128)S(1)} %fusion.54), kind=kOutput, calls=%fused_computation.95 | convolution fusion | flops 4860936192 | bytes 18874368 | tf_op jit(solution)/shard_map/secf,efd->secd/dot_general | solution.py:235
  252.2 20.2 %all-to-all-start = ((bf16[4,256,768]{2,1,0:T(8,128)(2,1)}), bf16[4,256,768]{2,1,0:T(8,128)(2,1)}, u32[]{:S(2)}, u32[]{:S(2)}) async-start(bf16[4,256,768]{2,1,0:T(8,128)(2,1)} %fusion.77), calls=%async_computation | async-start | bytes 3145728 | tf_op jit(solution)/shard_map/all_to_all | solution.py:238
  272.4 15.3 %fusion.6 = bf16[4,1,256,3072]{3,2,0,1:T(8,128)(2,1)S(1)} fusion(f32[4,256,3072]{2,1,0:T(8,128)} %copy-done.69, bf16[4,256,768]{2,1,0:T(8,128)(2,1)} %all-to-all-done.1, bf16[1,3072,768]{2,1,0:T(8,128)(2,1)} %param.24), kind=kOutput, calls=%fused_computation.14 | convolution fusion | flops 4894752768 | bytes 25165824 | tf_op jit(solution)/shard_map/secd,efd->secf/dot_general | solution.py:256
  287.8 8.7 %fusion.82 = bf16[4,256,768]{2,1,0:T(8,128)(2,1)} fusion(bf16[1,768,3072]{2,1,0:T(8,128)(2,1)} %param.23, bf16[4,1,256,3072]{3,2,0,1:T(8,128)(2,1)S(1)} %fusion.6), kind=kOutput, calls=%fused_computation.96 | convolution fusion | flops 4832624640 | bytes 12582912 | tf_op jit(solution)/shard_map/secf,edf->secd/dot_general | solution.py:261
  296.4 6.8 fusion.56
  312.4 12.0 %fusion.59 = bf16[1,3072,768]{2,1,0:T(8,128)(2,1)} fusion(bf16[4,256,768]{2,1,0:T(8,128)(2,1)} %all-to-all-done.1, f32[4,256,3072]{2,1,0:T(8,128)} %copy-done.69), kind=kOutput, calls=%fused_computation.72 | convolution fusion | flops 4862509056 | bytes 18874368 | tf_op jit(solution)/shard_map/secf,secd->efd/dot_general | solution.py:253
  329.4 20.3 %all-to-all-done.2 = bf16[4,256,768]{2,1,0:T(8,128)(2,1)} async-done(((bf16[4,256,768]{2,1,0:T(8,128)(2,1)}), bf16[4,256,768]{2,1,0:T(8,128)(2,1)}, u32[]{:S(2)}, u32[]{:S(2)}) %all-to-all-start.2) | async-done | bytes 1572896 | tf_op jit(solution)/shard_map/all_to_all | solution.py:264
  368.4 8.6 %fusion.110 = bf16[12,64,512]{2,1,0:T(8,128)(2,1)} fusion(bf16[512,12,64]{0,2,1:T(8,128)(2,1)} %bitcast.311, f32[12,512,512]{1,2,0:T(8,128)} %get-tuple-element.262, f32[12,512]{1,0:T(8,128)} %log_add_fusion, pred[512,512]{0,1:T(8,128)(4,1)} %get-tuple-element.244), kind=kOutput, calls=%fused_computation.132 | convolution fusion | flops 415629312 | bytes 14442496 | tf_op jit(solution)/shard_map/while/body/eval_jaxpr/hqk,qhd->khd/dot_general | solution.py:149
  376.9 7.8 %multiply_convert_fusion = bf16[12,512,512]{1,2,0:T(8,128)(2,1)S(1)} fusion(f32[12,512,512]{1,2,0:T(8,128)} %get-tuple-element.262, f32[12,512]{1,0:T(8,128)S(1)} %bitcast.331, f32[12,512]{1,0:T(8,128)S(1)} %copy-done.49, pred[512,512]{0,1:T(8,128)(4,1)S(1)} %copy-done.23, bf16[512,12,64]{0,2,1:T(8,128)(2,1)S(1)} %bitcast.312, ...), kind=kOutput, calls=%fused_computation.22 | convolution fusion | flops 421527552 | bytes 20758528 | tf_op jit(solution)/shard_map/while/body/eval_jaxpr/qhd,khd->hqk/dot_general | solution.py:119
  384.8 7.6 %multiply_convert_fusion.2 = bf16[12,512,512]{1,2,0:T(8,128)(2,1)S(1)} fusion(f32[12,512,512]{1,2,0:T(8,128)} %get-tuple-element.266, f32[12,512]{1,0:T(8,128)S(1)} %bitcast.332, f32[12,512]{1,0:T(8,128)S(1)} %copy-done.49, pred[512,512]{0,1:T(8,128)(4,1)} %copy-done.19, bf16[512,12,64]{0,2,1:T(8,128)(2,1)S(1)} %bitcast.313, bf16[512,12,64]{0,2,1:T(8,128)(2,1)} %bitcast.323), kind=kOutput, calls=%fused_computation.26 | convolution fusion | flops 421527552 | bytes 20758528 | tf_op jit(solution)/shard_map/while/body/eval_jaxpr/qhd,khd->hqk/dot_general | solution.py:119
  397.9 7.9 %multiply_convert_fusion.1 = bf16[12,512,512]{1,2,0:T(8,128)(2,1)S(1)} fusion(f32[12,512,512]{1,2,0:T(8,128)} %get-tuple-element.264, f32[12,512]{1,0:T(8,128)S(1)} %bitcast.333, f32[12,512]{1,0:T(8,128)S(1)} %copy-done.49, pred[512,512]{0,1:T(8,128)(4,1)} %get-tuple-element.245, bf16[512,12,64]{0,2,1:T(8,128)(2,1)S(1)} %bitcast.314, ...), kind=kOutput, calls=%fused_computation.24 | convolution fusion | flops 421527552 | bytes 20758528 | tf_op jit(solution)/shard_map/while/body/eval_jaxpr/qhd,khd->hqk/dot_general | solution.py:119
  416.1 6.1 fusion.30
  435.5 17.2 %collective-permute-done.6 = bf16[512,1536]{0,1:T(8,128)(2,1)} collective-permute-done((bf16[512,1536]{0,1:T(8,128)(2,1)}, bf16[512,1536]{0,1:T(8,128)(2,1)}, u32[]{:S(2)}, u32[]{:S(2)}) %collective-permute-start.6) | collective-permute-done | bytes 1572896 | tf_op jit(solution)/shard_map/ppermute | solution.py:40
  461.3 20.3 %all-reduce.8.cloned.1.call-done = (bf16[1,768,3072]{2,1,0:T(8,128)(2,1)}, bf16[1,3072,768]{2,1,0:T(8,128)(2,1)}) async-done(((bf16[1,768,3072]{2,1,0:T(8,128)(2,1)}, bf16[1,3072,768]{2,1,0:T(8,128)(2,1)}), (bf16[1,768,3072]{2,1,0:T(8,128)(2,1)}, bf16[1,3072,768]{2,1,0:T(8,128)(2,1)})) %all-reduce.8.cloned.1.call-update) | async-done | bytes 9437200 | tf_op jit(solution)/shard_map/psum | solution.py:327
  481.6 7.5 %convert_element_type.162 = f32[1,768,3072]{2,1,0:T(8,128)} convert(bf16[1,768,3072]{2,1,0:T(8,128)(2,1)} %get-tuple-element.192) | non-fusion elementwise | flops 2359296 | bytes 14155776 | tf_op jit(solution)/shard_map/convert_element_type | solution.py:327
  497.8 56.7 %all-reduce = (f32[768]{0:T(1024)}, f32[768]{0:T(1024)}, f32[768]{0:T(1024)}, f32[768]{0:T(1024)}) all-reduce(f32[768]{0:T(1024)} %get-tuple-element.167, f32[768]{0:T(1024)} %get-tuple-element.170, f32[768]{0:T(1024)S(1)} %get-tuple-element.165, f32[768]{0:T(1024)S(1)} %copy-done.52), channel_id=1, replica_groups=mesh['seq'=8,'exp'=4] {'seq','exp'}, use_global_device_ids=true, to_apply=%region_23.24 | all-reduce | flops 3072 | bytes 24576 | tf_op jit(solution)/shard_map/psum | solution.py:315
  559.8 129.0 %all-reduce.6.cloned.1.call-done = (f32[768,2304]{1,0:T(8,128)}, f32[768,768]{1,0:T(8,128)}) async-done(((f32[768,2304]{1,0:T(8,128)}, f32[768,768]{1,0:T(8,128)}), (f32[768,2304]{1,0:T(8,128)}, f32[768,768]{1,0:T(8,128)})) %all-reduce.6.cloned.1.call-update) | async-done | bytes 9437200 | tf_op jit(solution)/shard_map/psum | solution.py:315
  688.8 6.6 copy.136
  (258 shorter events, 184.9 us)
Async XLA Ops:
  10.2 9.5 %copy-start.61 = (s32[1,512]{1,0:T(1,128)S(1)}, s32[1,512]{1,0:T(1,128)}, u32[]{:S(2)}) copy-start(s32[1,512]{1,0:T(1,128)} %param.14) | copy-start | bytes 6148
  16.2 43.2 %collective-permute-start = (bf16[512,1536]{1,0:T(8,128)(2,1)}, bf16[512,1536]{1,0:T(8,128)(2,1)}, u32[]{:S(2)}, u32[]{:S(2)}) collective-permute-start(bf16[512,1536]{1,0:T(8,128)(2,1)} %slice.67), channel_id=1, source_target_pairs={{0,4},{4,8},{8,12},{12,16},{16,20},{20,24},{24,28},{1,5},{5,9},{9,... | collective-permute-start | bytes 4718600 | tf_op jit(solution)/shard_map/ppermute | solution.py:40
  48.4 15.8 %copy-start.60 = (s32[4]{0:T(128)S(1)}, s32[4]{0:T(128)}, u32[]{:S(2)}) copy-start(s32[4]{0:T(128)} %copy-done.59) | copy-start | bytes 52
  59.4 14.0 %copy-start.19 = (pred[512,512]{0,1:T(8,128)(4,1)}, pred[512,512]{0,1:T(8,128)(4,1)S(1)}, u32[]{:S(2)}) copy-start(pred[512,512]{0,1:T(8,128)(4,1)S(1)} %get-tuple-element.243) | copy-start | bytes 786436
  59.4 29.8 %collective-permute-start.1 = (bf16[512,1536]{1,0:T(8,128)(2,1)}, bf16[512,1536]{1,0:T(8,128)(2,1)}, u32[]{:S(2)}, u32[]{:S(2)}) collective-permute-start(bf16[512,1536]{1,0:T(8,128)(2,1)} %collective-permute-done), channel_id=1, source_target_pairs={{0,4},{4,8},{8,12},{12,16},{16,20},{20,24},{24,28},{1,5},{5,9},{9,... | collective-permute-start | bytes 4718600 | tf_op jit(solution)/shard_map/ppermute | solution.py:40
  105.2 28.2 %slice-start = ((s8[12582912]{0:T(1024)(128)(4,1)}), s8[4194304]{0:T(1024)(128)(4,1)S(1)}, s32[]{:S(2)}) async-start(s8[12582912]{0:T(1024)(128)(4,1)} %bitcast.290), calls=%async_computation.5 | async-start | bytes 8388608
  105.2 28.2 %slice-start.1 = ((s8[12582912]{0:T(1024)(128)(4,1)}), s8[4194304]{0:T(1024)(128)(4,1)S(1)}, s32[]{:S(2)}) async-start(s8[12582912]{0:T(1024)(128)(4,1)} %bitcast.290), calls=%async_computation.6 | async-start | bytes 8388608
  112.5 36.6 %copy-start.37 = (f32[12,512]{1,0:T(8,128)}, f32[12,512]{1,0:T(8,128)S(1)}, u32[]{:S(2)}) copy-start(f32[12,512]{1,0:T(8,128)S(1)} %fusion.13) | copy-start | bytes 73732
  112.5 20.9 %slice-start.2 = ((s8[12582912]{0:T(1024)(128)(4,1)}), s8[4194304]{0:T(1024)(128)(4,1)S(1)}, s32[]{:S(2)}) async-start(s8[12582912]{0:T(1024)(128)(4,1)} %bitcast.290), calls=%async_computation.7 | async-start | bytes 8388608
  137.0 12.1 %copy-start.38 = (f32[12,512]{1,0:T(8,128)}, f32[12,512]{1,0:T(8,128)S(1)}, u32[]{:S(2)}) copy-start(f32[12,512]{1,0:T(8,128)S(1)} %fusion.11) | copy-start | bytes 73732
  149.1 8.9 %copy-start.39 = (f32[12,512]{1,0:T(8,128)}, f32[12,512]{1,0:T(8,128)S(1)}, u32[]{:S(2)}) copy-start(f32[12,512]{1,0:T(8,128)S(1)} %fusion.15) | copy-start | bytes 73732
  149.2 8.8 %copy-start.10 = (bf16[1,512,768]{2,1,0:T(8,128)(2,1)S(1)}, bf16[1,512,768]{2,1,0:T(8,128)(2,1)}, u32[]{:S(2)}) copy-start(bf16[1,512,768]{2,1,0:T(8,128)(2,1)} %param.13) | copy-start | bytes 2359300
  149.2 8.8 %copy-start.64 = (bf16[768,768]{1,0:T(8,128)(2,1)S(1)}, bf16[768,768]{1,0:T(8,128)(2,1)}, u32[]{:S(2)}) copy-start(bf16[768,768]{1,0:T(8,128)(2,1)} %param.22) | copy-start | bytes 3538948
  174.3 20.7 %collective-permute-start.2 = (bf16[1,256,768]{2,1,0:T(8,128)(2,1)}, bf16[1,256,768]{2,1,0:T(8,128)(2,1)}, u32[]{:S(2)}, u32[]{:S(2)}) collective-permute-start(bf16[1,256,768]{2,1,0:T(8,128)(2,1)} %get-tuple-element.218), channel_id=1, source_target_pairs={{0,1},{1,0},{2,3},{3,2},{4,5},{5,4},{6,7},{7,6},{8,9},{9,8},{10,11... | collective-permute-start | bytes 1179656 | tf_op jit(solution)/shard_map/ppermute | solution.py:31
  175.9 29.9 %collective-permute-start.3 = (bf16[1,256,768]{2,1,0:T(8,128)(2,1)}, bf16[1,256,768]{2,1,0:T(8,128)(2,1)}, u32[]{:S(2)}, u32[]{:S(2)}) collective-permute-start(bf16[1,256,768]{2,1,0:T(8,128)(2,1)} %get-tuple-element.217), channel_id=1, source_target_pairs={{0,2},{1,3},{2,0},{3,1},{4,6},{5,7},{6,4},{7,5},{8,10},{9,11},{10,... | collective-permute-start | bytes 1179656 | tf_op jit(solution)/shard_map/ppermute | solution.py:31
  178.6 73.6 %all-to-all-start.1 = ((bf16[4,256,768]{2,1,0:T(8,128)(2,1)}), bf16[4,256,768]{2,1,0:T(8,128)(2,1)}, u32[]{:S(2)}, u32[]{:S(2)}) async-start(bf16[4,256,768]{2,1,0:T(8,128)(2,1)} %get-tuple-element.246), calls=%async_computation.1 | async-start | bytes 3145728 | tf_op jit(solution)/shard_map/all_to_all | solution.py:250
  183.0 45.8 %collective-permute-start.4 = (bf16[1,256,768]{2,1,0:T(8,128)(2,1)}, bf16[1,256,768]{2,1,0:T(8,128)(2,1)S(1)}, u32[]{:S(2)}, u32[]{:S(2)}) collective-permute-start(bf16[1,256,768]{2,1,0:T(8,128)(2,1)} %get-tuple-element.216), channel_id=1, source_target_pairs={{0,3},{1,2},{2,1},{3,0},{4,7},{5,6},{6,5},{7,4},{8,11},{9,10},{10,... | collective-permute-start | bytes 1179656 | tf_op jit(solution)/shard_map/ppermute | solution.py:31
  252.2 55.9 %all-to-all-start = ((bf16[4,256,768]{2,1,0:T(8,128)(2,1)}), bf16[4,256,768]{2,1,0:T(8,128)(2,1)}, u32[]{:S(2)}, u32[]{:S(2)}) async-start(bf16[4,256,768]{2,1,0:T(8,128)(2,1)} %fusion.77), calls=%async_computation | async-start | bytes 3145728 | tf_op jit(solution)/shard_map/all_to_all | solution.py:238
  308.0 41.6 %all-to-all-start.2 = ((bf16[4,256,768]{2,1,0:T(8,128)(2,1)}), bf16[4,256,768]{2,1,0:T(8,128)(2,1)}, u32[]{:S(2)}, u32[]{:S(2)}) async-start(bf16[4,256,768]{2,1,0:T(8,128)(2,1)} %fusion.82), calls=%async_computation.2 | async-start | bytes 3145728 | tf_op jit(solution)/shard_map/all_to_all | solution.py:264
  312.4 169.2 %all-reduce.8.cloned.1.call-start = ((), (), s32[]{:S(2)}) async-start(), calls=%async_computation.4 | async-start | bytes 18874368 | tf_op jit(solution)/shard_map/psum | solution.py:327
  324.5 364.3 %all-reduce.6.cloned.1.call-start = ((), (), s32[]{:S(2)}) async-start(), calls=%async_computation.3 | async-start | bytes 18874368 | tf_op jit(solution)/shard_map/psum | solution.py:315
  409.1 13.1 %collective-permute-start.5 = (bf16[512,1536]{0,1:T(8,128)(2,1)}, bf16[512,1536]{0,1:T(8,128)(2,1)}, u32[]{:S(2)}, u32[]{:S(2)}) collective-permute-start(bf16[512,1536]{0,1:T(8,128)(2,1)} %pad_maximum_fusion.1), channel_id=1, source_target_pairs={{4,0},{8,4},{12,8},{16,12},{20,16},{24,20},{28,24},{5,1},{9,5},{13... | collective-permute-start | bytes 4718600 | tf_op jit(solution)/shard_map/ppermute | solution.py:40
  416.1 15.7 %slice-start.3 = ((s8[12582912]{0:T(1024)(128)(4,1)}), s8[4194304]{0:T(1024)(128)(4,1)S(1)}, s32[]{:S(2)}) async-start(s8[12582912]{0:T(1024)(128)(4,1)} %bitcast.292), calls=%async_computation.8 | async-start | bytes 8388608
  416.1 15.7 %slice-start.4 = ((s8[12582912]{0:T(1024)(128)(4,1)}), s8[4194304]{0:T(1024)(128)(4,1)S(1)}, s32[]{:S(2)}) async-start(s8[12582912]{0:T(1024)(128)(4,1)} %bitcast.292), calls=%async_computation.9 | async-start | bytes 8388608
  425.6 27.1 %collective-permute-start.6 = (bf16[512,1536]{0,1:T(8,128)(2,1)}, bf16[512,1536]{0,1:T(8,128)(2,1)}, u32[]{:S(2)}, u32[]{:S(2)}) collective-permute-start(bf16[512,1536]{0,1:T(8,128)(2,1)} %fusion.64), channel_id=1, source_target_pairs={{4,0},{8,4},{12,8},{16,12},{20,16},{24,20},{28,24},{5,1},{9,5},{13... | collective-permute-start | bytes 4718600 | tf_op jit(solution)/shard_map/ppermute | solution.py:40
  431.8 20.9 %copy-start.14 = (f32[12,64,512]{2,1,0:T(8,128)S(1)}, f32[12,64,512]{2,1,0:T(8,128)}, u32[]{:S(2)}) copy-start(f32[12,64,512]{2,1,0:T(8,128)} %convolution_multiply_fusion) | copy-start | bytes 4718596
  435.4 20.5 %copy-start.11 = (bf16[1,512,768]{2,1,0:T(8,128)(2,1)S(1)}, bf16[1,512,768]{2,1,0:T(8,128)(2,1)}, u32[]{:S(2)}) copy-start(bf16[1,512,768]{2,1,0:T(8,128)(2,1)} %param.13) | copy-start | bytes 2359300
  435.4 20.5 %copy-start.34 = (bf16[12,64,512]{2,1,0:T(8,128)(2,1)S(1)}, bf16[12,64,512]{2,1,0:T(8,128)(2,1)}, u32[]{:S(2)}) copy-start(bf16[12,64,512]{2,1,0:T(8,128)(2,1)} %multiply_convert_fusion.4) | copy-start | bytes 2359300
  435.4 20.5 %copy-start.51 = (f32[512]{0:T(512)S(1)}, f32[512]{0:T(512)}, u32[]{:S(2)}) copy-start(f32[512]{0:T(512)} %copy-done.50) | copy-start | bytes 6148
  435.5 20.5 %copy-start.54 = (f32[512]{0:T(512)S(1)}, f32[512]{0:T(512)}, u32[]{:S(2)}) copy-start(f32[512]{0:T(512)} %copy-done.53) | copy-start | bytes 6148
  435.5 20.5 %copy-start.57 = (f32[768]{0:T(1024)S(1)}, f32[768]{0:T(1024)}, u32[]{:S(2)}) copy-start(f32[768]{0:T(1024)} %param.17) | copy-start | bytes 9220
  435.5 20.4 %copy-start.66 = (f32[768]{0:T(1024)S(1)}, f32[768]{0:T(1024)}, u32[]{:S(2)}) copy-start(f32[768]{0:T(1024)} %param.18) | copy-start | bytes 9220
  (56 other events, 289.2 us)
Sparse Core Ops, SparseCore 0:
  324.6 156.8 all-reduce.7
  489.1 199.6 all-reduce.5
